TPU v7x, 32 devices: a whole 2x2x4 slice. The times are simulated.
32 devices in a mesh: dp: 8 (over z, x), tensor: 4 (over y, core).
Axes of the slice: x: 2, y: 2, z: 4, core: 2. Of those that a mesh axis runs over, the one named last changes fastest.
Arguments:
- layer_in: bfloat16 [16384, 1024], P(('dp', 'tensor')), may hold values from -6 to 6
- cotangent: bfloat16 [16384, 1024], P(('dp', 'tensor')), may hold values from -6 to 6
- lengths: int32 [8], P('dp'), may hold values from 256 to 2048, as said below
- languages: int32 [8], P('dp'), may hold values from 0 to 45
- lang_weight: float32 [46], replicated, may hold values from 0.3 to 3
- ln1_gain: float32 [1024], replicated, may hold values from 0.5 to 1.5
- ln1_bias: float32 [1024], replicated, may hold values from -2.5 to 2.5
- w_qkv: bfloat16 [1024, 3072], P(None, 'tensor'), may hold values from -0.1875 to 0.1875
- b_qv: float32 [2048], P('tensor'), may hold values from -2.5 to 2.5
- w_out: bfloat16 [1024, 1024], P('tensor'), may hold values from -1.5 to 1.5
- b_out: float32 [1024], replicated, may hold values from -2.5 to 2.5
- ln2_gain: float32 [1024], replicated, may hold values from 0.5 to 1.5
- ln2_bias: float32 [1024], replicated, may hold values from -2.5 to 2.5
- w_up: bfloat16 [1024, 4096], P(None, 'tensor'), may hold values from -0.1875 to 0.1875
- b_up: float32 [4096], P('tensor'), may hold values from -2.5 to 2.5
- w_down: bfloat16 [4096, 1024], P('tensor'), may hold values from -0.09375 to 0.09375
- b_down: float32 [1024], replicated, may hold values from -2.5 to 2.5
Outputs:
- output: bfloat16 [16384, 1024], P(('dp', 'tensor'))
- grad_x: bfloat16 [16384, 1024], P(('dp', 'tensor'))
- g_ln1_gain: float32 [1024], replicated
- g_ln1_bias: float32 [1024], replicated
- g_w_qkv: float32 [1024, 3072], P(None, 'tensor')
- g_b_qv: float32 [2048], P('tensor')
- g_w_out: float32 [1024, 1024], P('tensor')
- g_b_out: float32 [1024], replicated
- g_ln2_gain: float32 [1024], replicated
- g_ln2_bias: float32 [1024], replicated
- g_w_up: float32 [1024, 4096], P(None, 'tensor')
- g_b_up: float32 [4096], P('tensor')
- g_w_down: float32 [4096, 1024], P('tensor')
- g_b_down: float32 [1024], replicated
Inputs may be any that keep to these rules, and one draw needn't show every extreme that they name: `lengths`: rows of languages 0 to 7 have all 2048 tokens; some row has 2048 tokens and some row 256.
All inputs are finite; a program needn't handle non-finite values.
Results may differ from a plain program's by a relative error of at most 0.019.
Values may be sent and summed in bfloat16 or wider, within the bound.
No kernel may reach another device: no remote copies, remote signals or barrier semaphores. Data moves between devices by JAX's collectives and lax.ppermute only.
A program may use at most 192 MiB of HBM per device.

v0:
```python
import jax
import jax.numpy as jnp
from jax import lax
from jax.sharding import PartitionSpec as P

HEADS = 16
HD = 64
eps = 1e-05
block_most = 512


def layer_norm(values, gain, bias):
    centre = jnp.mean(values, axis=-1, keepdims=True)
    shifted = values - centre
    spread = jnp.mean(shifted * shifted, axis=-1, keepdims=True)
    factor = lax.rsqrt(spread + eps)
    unit_rows = shifted * factor
    return (unit_rows * gain + bias, unit_rows, factor)


def norm_back(grad_rows, unit_rows, factor, gain):
    scaled = grad_rows * gain
    inner = jnp.mean(scaled * unit_rows, axis=-1, keepdims=True)
    return factor * (scaled - jnp.mean(scaled, axis=-1, keepdims=True) - unit_rows * inner)


def cross_rows(left, right):
    return lax.dot_general(
        left, right, (((0,), (0,)), ((), ())), preferred_element_type=jnp.float32
    )


def times_trans(left, right):
    return lax.dot_general(
        left, right, (((1,), (1,)), ((), ())), preferred_element_type=jnp.float32
    )


def block_rows():
    return block_most


def qkv_bias(pairs):
    return jnp.stack([pairs[:, 0], jnp.zeros_like(pairs[:, 0]), pairs[:, 1]], axis=1)


def masked_scores(query_block, keys, start, length, slopes):
    query_pos = start + jnp.arange(query_block.shape[1], dtype=jnp.int32)
    key_pos = jnp.arange(keys.shape[1], dtype=jnp.int32)
    scores = jnp.einsum(
        "hqe,hke->hqk", query_block, keys, preferred_element_type=jnp.float32
    ) * keys.shape[2] ** (-0.5)
    offsets = (key_pos[None, :] - query_pos[:, None]).astype(jnp.float32)
    scores = scores + slopes[:, None, None] * offsets[None]
    allowed = (key_pos[None, :] <= query_pos[:, None]) & (key_pos[None, :] < length)
    return jnp.where(allowed[None], scores, -jnp.inf)


def attend_forward(query, keys, values, length, slopes):
    span = query.shape[1]
    block = block_rows()

    def forward_block(start):
        query_block = lax.dynamic_slice_in_dim(query, start, block, 1)
        scores = masked_scores(query_block, keys, start, length, slopes)
        highest = jnp.max(scores, axis=-1, keepdims=True)
        expos = jnp.exp(scores - highest)
        denom = jnp.sum(expos, axis=-1, keepdims=True)
        probs_b = (expos / denom).astype(jnp.bfloat16)
        result = jnp.einsum("hqk,hke->hqe", probs_b, values, preferred_element_type=jnp.float32)
        return (result, (highest + jnp.log(denom))[..., 0])

    starts = jnp.arange(span // block, dtype=jnp.int32) * block
    results, log_total = lax.map(forward_block, starts)
    heads_count = query.shape[0]
    return (
        results.transpose(1, 0, 2, 3).reshape(query.shape),
        log_total.transpose(1, 0, 2).reshape(heads_count, span),
    )


def attend_backward(query, keys, values, grad_heads, log_total, length, slopes):
    span = query.shape[1]
    block = block_rows()
    scale = keys.shape[2] ** (-0.5)

    def backward_block(carry, start):
        grad_keys, grad_values = carry
        query_block = lax.dynamic_slice_in_dim(query, start, block, 1)
        grad_block = lax.dynamic_slice_in_dim(grad_heads, start, block, 1)
        log_block = lax.dynamic_slice_in_dim(log_total, start, block, 1)
        scores = masked_scores(query_block, keys, start, length, slopes)
        probs = jnp.exp(scores - log_block[..., None])
        grad_probs = jnp.einsum(
            "hqe,hke->hqk", grad_block, values, preferred_element_type=jnp.float32
        )
        grad_scores = (
            probs * (grad_probs - jnp.sum(probs * grad_probs, axis=-1, keepdims=True))
        ).astype(jnp.bfloat16)
        grad_query = (
            jnp.einsum("hqk,hke->hqe", grad_scores, keys, preferred_element_type=jnp.float32)
            * scale
        )
        grad_keys = (
            grad_keys
            + jnp.einsum(
                "hqk,hqe->hke", grad_scores, query_block, preferred_element_type=jnp.float32
            )
            * scale
        )
        grad_values = grad_values + jnp.einsum(
            "hqk,hqe->hke",
            probs.astype(jnp.bfloat16),
            grad_block,
            preferred_element_type=jnp.float32,
        )
        return ((grad_keys, grad_values), grad_query)

    starts = jnp.arange(span // block, dtype=jnp.int32) * block
    empty = jnp.zeros(keys.shape, jnp.float32)
    (grad_keys, grad_values), grad_query = lax.scan(backward_block, (empty, empty), starts)
    return (grad_query.transpose(1, 0, 2, 3).reshape(query.shape), grad_keys, grad_values)


def body(
    layer_in,
    cotangent,
    lengths,
    languages,
    lang_weight,
    ln1_gain,
    ln1_bias,
    w_qkv,
    b_qv,
    w_out,
    b_out,
    ln2_gain,
    ln2_bias,
    w_up,
    b_up,
    w_down,
    b_down,
):
    groups = lax.axis_size("tensor")
    place = lax.axis_index("tensor")
    own_rows = layer_in.shape[0]
    all_rows = own_rows * groups
    seq_count = lengths.shape[0]
    seq_len = all_rows // seq_count
    head_dim = HD
    local_heads = w_out.shape[0] // head_dim
    head_ids = (place * local_heads + jnp.arange(local_heads, dtype=jnp.int32)).astype(jnp.float32)
    slopes = jnp.exp2(-8.0 * (head_ids + 1.0) / HEADS)
    in_float = layer_in.astype(jnp.float32)
    normed1, unit1, factor1 = layer_norm(in_float, ln1_gain, ln1_bias)
    normed1_b = normed1.astype(jnp.bfloat16)
    mixed = jnp.dot(
        lax.all_gather(normed1_b, "tensor", axis=0, tiled=True),
        w_qkv,
        preferred_element_type=jnp.float32,
    )
    bias_three = qkv_bias(b_qv.reshape(local_heads, 2, head_dim))
    mixed_b = (mixed.reshape(all_rows, local_heads, 3, head_dim) + bias_three[None]).astype(
        jnp.bfloat16
    )
    per_seq = mixed_b.reshape(seq_count, seq_len, local_heads, 3, head_dim).transpose(0, 3, 2, 1, 4)

    def forward_seq(item):
        parts, length = item
        return attend_forward(parts[0], parts[1], parts[2], length, slopes)

    heads_out, log_total = lax.map(forward_seq, (per_seq, lengths))
    heads_b = (
        heads_out.astype(jnp.bfloat16)
        .transpose(0, 2, 1, 3)
        .reshape(all_rows, local_heads * head_dim)
    )
    attn_sum = lax.psum_scatter(
        jnp.dot(heads_b, w_out, preferred_element_type=jnp.float32).astype(jnp.bfloat16),
        "tensor",
        scatter_dimension=0,
        tiled=True,
    ).astype(jnp.float32)
    middle = in_float + attn_sum + b_out
    normed2, unit2, factor2 = layer_norm(middle, ln2_gain, ln2_bias)
    normed2_b = normed2.astype(jnp.bfloat16)
    pre_act = (
        jnp.dot(
            lax.all_gather(normed2_b, "tensor", axis=0, tiled=True),
            w_up,
            preferred_element_type=jnp.float32,
        )
        + b_up
    )
    gelu_out, gelu_pull = jax.vjp(lambda inputs: jax.nn.gelu(inputs, approximate=True), pre_act)
    active_b = gelu_out.astype(jnp.bfloat16)
    output = (
        middle
        + lax.psum_scatter(
            jnp.dot(active_b, w_down, preferred_element_type=jnp.float32).astype(jnp.bfloat16),
            "tensor",
            scatter_dimension=0,
            tiled=True,
        ).astype(jnp.float32)
        + b_down
    )
    row_ids = place * own_rows + jnp.arange(own_rows, dtype=jnp.int32)
    seq_ids = row_ids // seq_len
    positions = row_ids - seq_ids * seq_len
    seq_hit = seq_ids[:, None] == jnp.arange(seq_count, dtype=jnp.int32)[None, :]
    row_length = jnp.sum(jnp.where(seq_hit, lengths[None, :], 0), axis=1)
    row_lang = jnp.sum(jnp.where(seq_hit, languages[None, :], 0), axis=1)
    lang_hit = row_lang[:, None] == jnp.arange(lang_weight.shape[0], dtype=jnp.int32)[None, :]
    row_weight = jnp.sum(jnp.where(lang_hit, lang_weight[None, :], 0.0), axis=1)
    live = jnp.where(positions < row_length, row_weight, 0.0)
    grad_top = cotangent.astype(jnp.float32) * live[:, None]
    g_b_down = jnp.sum(grad_top, axis=0)
    grad_full = lax.all_gather(grad_top.astype(jnp.bfloat16), "tensor", axis=0, tiled=True)
    g_w_down = cross_rows(active_b, grad_full)
    grad_active = times_trans(grad_full, w_down)
    grad_pre_b = gelu_pull(grad_active)[0].astype(jnp.bfloat16)
    g_b_up = jnp.sum(grad_pre_b.astype(jnp.float32), axis=0)
    rows_here = grad_pre_b
    g_w_up = cross_rows(lax.all_gather(normed2_b, "tensor", axis=0, tiled=True), rows_here)
    grad_norm2 = lax.psum_scatter(
        times_trans(grad_pre_b, w_up).astype(jnp.bfloat16),
        "tensor",
        scatter_dimension=0,
        tiled=True,
    ).astype(jnp.float32)
    g_ln2_gain = jnp.sum(grad_norm2 * unit2, axis=0)
    g_ln2_bias = jnp.sum(grad_norm2, axis=0)
    grad_middle = grad_top + norm_back(grad_norm2, unit2, factor2, ln2_gain)
    g_b_out = jnp.sum(grad_middle, axis=0)
    grad_mid_b = grad_middle.astype(jnp.bfloat16)
    grad_mid_full = lax.all_gather(grad_mid_b, "tensor", axis=0, tiled=True)
    g_w_out = cross_rows(heads_b, grad_mid_full)
    grad_heads_b = times_trans(grad_mid_full, w_out).astype(jnp.bfloat16)
    grad_seq = grad_heads_b.reshape(seq_count, seq_len, local_heads, head_dim).transpose(0, 2, 1, 3)

    def backward_seq(item):
        parts, grad_part, log_part, length = item
        return attend_backward(parts[0], parts[1], parts[2], grad_part, log_part, length, slopes)

    grad_query, grad_key, grad_value = lax.map(
        backward_seq, (per_seq, grad_seq, log_total, lengths)
    )
    grad_parts = jnp.stack([grad_query, grad_key, grad_value], axis=1)
    grad_mixed_b = (
        grad_parts.transpose(0, 3, 2, 1, 4)
        .reshape(all_rows, local_heads * 3 * head_dim)
        .astype(jnp.bfloat16)
    )
    column_sums = jnp.sum(grad_mixed_b.astype(jnp.float32), axis=0).reshape(
        local_heads, 3, head_dim
    )
    g_b_qv = jnp.stack([column_sums[:, 0], column_sums[:, 2]], axis=1).reshape(-1)
    rows_here = grad_mixed_b
    g_w_qkv = cross_rows(lax.all_gather(normed1_b, "tensor", axis=0, tiled=True), rows_here)
    grad_norm1 = lax.psum_scatter(
        times_trans(grad_mixed_b, w_qkv).astype(jnp.bfloat16),
        "tensor",
        scatter_dimension=0,
        tiled=True,
    ).astype(jnp.float32)
    g_ln1_gain = jnp.sum(grad_norm1 * unit1, axis=0)
    g_ln1_bias = jnp.sum(grad_norm1, axis=0)
    grad_input = grad_middle + norm_back(grad_norm1, unit1, factor1, ln1_gain)
    weights = (
        lax.psum(g_w_qkv.astype(jnp.bfloat16), "dp").astype(jnp.float32),
        lax.psum(g_b_qv.astype(jnp.bfloat16), "dp").astype(jnp.float32),
        lax.psum(g_w_out.astype(jnp.bfloat16), "dp").astype(jnp.float32),
        lax.psum(g_w_up.astype(jnp.bfloat16), "dp").astype(jnp.float32),
        lax.psum(g_b_up.astype(jnp.bfloat16), "dp").astype(jnp.float32),
        lax.psum(g_w_down.astype(jnp.bfloat16), "dp").astype(jnp.float32),
    )
    shared = lax.psum(
        (g_ln1_gain, g_ln1_bias, g_b_out, g_ln2_gain, g_ln2_bias, g_b_down), ("dp", "tensor")
    )
    return (
        output.astype(jnp.bfloat16),
        grad_input.astype(jnp.bfloat16),
        shared[0],
        shared[1],
        weights[0],
        weights[1],
        weights[2],
        shared[2],
        shared[3],
        shared[4],
        weights[3],
        weights[4],
        weights[5],
        shared[5],
    )


def solution(mesh):
    in_specs = (
        P(("dp", "tensor"), None),
        P(("dp", "tensor"), None),
        P("dp"),
        P("dp"),
        P(),
        P(),
        P(),
        P(None, "tensor"),
        P("tensor"),
        P("tensor", None),
        P(),
        P(),
        P(),
        P(None, "tensor"),
        P("tensor"),
        P("tensor", None),
        P(),
    )
    out_specs = (
        P(("dp", "tensor"), None),
        P(("dp", "tensor"), None),
        P(),
        P(),
        P(None, "tensor"),
        P("tensor"),
        P("tensor", None),
        P(),
        P(),
        P(),
        P(None, "tensor"),
        P("tensor"),
        P("tensor", None),
        P(),
    )
    return jax.shard_map(body, mesh=mesh, in_specs=in_specs, out_specs=out_specs, check_vma=False)
```

profile of v0, /device:TPU:0, one launch (start us, length us, event | category | flops | bytes accessed | tf_op | source)
XLA Modules:
  0.0 1035.9 jit_solution(2467794752946454012)
XLA Ops:
  14.1 37.0 %all-gather.5.cloned.1.call-done = bf16[2048,1024]{1,0:T(8,128)(2,1)} async-done(((bf16[512,1024]{1,0:T(8,128)(2,1)}), bf16[2048,1024]{1,0:T(8,128)(2,1)}) %all-gather.5.cloned.1.call-update) | async-done | bytes 4194320 | tf_op jit(solution)/shard_map/all_gather | solution.py:158
  60.2 106.7 %while.48 = (s32[]{:T(128)}, bf16[4,4,512,64]{2,3,1,0:T(8,128)(2,1)}, f32[4,4,512]{2,1,0:T(4,128)S(1)}, s32[4]{0:T(128)S(1)}, s32[]{:T(128)}, /*index=5*/bf16[4,...) while((s32[]{:T(128)}, ...), condition=%wide.region_5.6_spmd.clone, body=%wide.region_2.5_spmd.clone.sunk | while | flops 1153434112 | bytes 99428696 | solution.py:74
  177.4 44.6 %reduce-scatter.5.cloned.1.call-done = bf16[512,1024]{1,0:T(8,128)(2,1)} async-done(((bf16[2048,1024]{1,0:T(8,128)(2,1)}), bf16[512,1024]{1,0:T(8,128)(2,1)}) %reduce-scatter.5.cloned.1.call-update) | async-done | bytes 1048592 | tf_op jit(solution)/shard_map/reduce_scatter | solution.py:178
  231.2 30.6 %all-gather.7.cloned.1.call-done = bf16[2048,1024]{1,0:T(8,128)(2,1)} async-done(((bf16[512,1024]{1,0:T(8,128)(2,1)}), bf16[2048,1024]{1,0:T(8,128)(2,1)}) %all-gather.7.cloned.1.call-update) | async-done | bytes 4194320 | tf_op jit(solution)/shard_map/all_gather | solution.py:189
  261.8 11.4 %fusion.83 = f32[2048,1024]{1,0:T(8,128)} fusion(bf16[2048,1024]{1,0:T(8,128)(2,1)} %all-gather.7.cloned.1.call-done, bf16[1024,1024]{1,0:T(8,128)(2,1)} %param.34), kind=kOutput, calls=%fused_computation.151 | convolution fusion | flops 4294967296 | bytes 14680064 | tf_op jit(solution)/shard_map/dot_general | solution.py:188
  273.2 25.2 %all-gather.9.cloned.1.call-done = bf16[2048,1024]{1,0:T(8,128)(2,1)} async-done(((bf16[512,1024]{1,0:T(8,128)(2,1)}), bf16[2048,1024]{1,0:T(8,128)(2,1)}) %all-gather.9.cloned.1.call-update) | async-done | bytes 4194320 | tf_op jit(solution)/shard_map/all_gather | solution.py:218
  298.4 13.8 %fusion.76 = (bf16[1024]{0:T(1024)(128)(2,1)}, bf16[2048,1024]{1,0:T(8,128)(2,1)S(1)}) fusion(f32[2048,1024]{1,0:T(8,128)} %fusion.83, f32[1024]{0:T(1024)S(1)} %copy-done.50, bf16[2048,1024]{1,0:T(8,128)(2,1)} %all-gather.9.cloned.1.call-done, bf16[1024,1024]{1,0:T(8,128)(2,1)S(1)} %copy-done), kind=kOutput, calls=%fused_computation.146 | convolution fusion | flops 4341103616 | bytes 18880512 | tf_op jit(solution)/shard_map/dot_general | solution.py:34
  320.4 11.2 %convolution_convert_fusion.3 = bf16[2048,1024]{1,0:T(8,128)(2,1)} fusion(bf16[1024,1024]{1,0:T(8,128)(2,1)S(1)} %copy-done, f32[2048,1024]{1,0:T(8,128)} %fusion.83, f32[1024]{0:T(1024)S(1)} %copy-done.50), kind=kOutput, calls=%fused_computation.65 | convolution fusion | flops 4318035968 | bytes 14684160 | tf_op jit(solution)/shard_map/dot_general | solution.py:200
  331.7 33.4 %reduce-scatter.9.cloned.1.call-done = bf16[512,1024]{1,0:T(8,128)(2,1)} async-done(((bf16[2048,1024]{1,0:T(8,128)(2,1)}), bf16[512,1024]{1,0:T(8,128)(2,1)}) %reduce-scatter.9.cloned.1.call-update) | async-done | bytes 1048592 | tf_op jit(solution)/shard_map/reduce_scatter | solution.py:225
  368.1 44.5 %reduce-scatter.7.cloned.1.call-done = bf16[512,1024]{1,0:T(8,128)(2,1)} async-done(((bf16[2048,1024]{1,0:T(8,128)(2,1)}), bf16[512,1024]{1,0:T(8,128)(2,1)}) %reduce-scatter.7.cloned.1.call-update) | async-done | bytes 1048592 | tf_op jit(solution)/shard_map/reduce_scatter | solution.py:199
  440.1 14.0 %all-gather.11.cloned.1.call-done = bf16[2048,1024]{1,0:T(8,128)(2,1)} async-done(((bf16[512,1024]{1,0:T(8,128)(2,1)}), bf16[2048,1024]{1,0:T(8,128)(2,1)}) %all-gather.11.cloned.1.call-update) | async-done | bytes 4194320 | tf_op jit(solution)/shard_map/all_gather | solution.py:236
  459.6 244.7 %while.49 = (s32[]{:T(128)}, f32[4,2048,64]{1,2,0:T(8,128)}, f32[4,2048,64]{1,2,0:T(8,128)}, bf16[4,4,512,64]{2,3,1,0:T(8,128)(2,1)}, s32[4]{0:T(128)S(1)}, /*in...) while((s32[]{:T(128)}, f32[4,2048,64]{1,2,0:T(8,128)}, ...), condition=%wide.region_16.17_spmd.clone, body=%wide.region_14.16_spmd.clone.sunk | while | flops 2737439232 | bytes 296274944 | solution.py:121
  474.2 14.5 %multiply_reduce_fusion.3 = (f32[4,512]{1,0:T(4,128)S(1)}, f32[4,512,2048]{2,1,0:T(8,128)}) fusion(f32[4,512,2048]{2,1,0:T(8,128)} %fusion.148, f32[4,512]{1,0:T(4,128)S(1)} %constant_dynamic-slice_fusion.2, f32[512,2048]{1,0:T(8,128)S(1)} %subtract_convert_fusion.5, f32[4]{0:T(128)S(1)} %multiply_exponential_fusion.5, ...), kind=kOutput, calls=%fused_computation.23.clone.1 | convolution fusion | flops 566228992 | bytes 40124932 | tf_op jit(solution)/shard_map/while/body/eval_jaxpr/while/body/eval_jaxpr/hqe,hke->hqk/dot_general | solution.py:50
  488.6 15.0 %multiply_convert_fusion.5 = bf16[4,512,2048]{2,1,0:T(8,128)(2,1)} fusion(f32[4,512,2048]{2,1,0:T(8,128)} %get-tuple-element.456, f32[4,512,2048]{2,1,0:T(8,128)} %fusion.148, f32[4,512]{1,0:T(4,128)S(1)} %get-tuple-element.457), kind=kLoop, calls=%fused_computation.22.clone.1 | loop fusion | flops 12582912 | bytes 41951232 | tf_op jit(solution)/shard_map/while/body/eval_jaxpr/while/body/eval_jaxpr/convert_element_type | solution.py:99
  535.2 14.5 %multiply_reduce_fusion.3 = (f32[4,512]{1,0:T(4,128)S(1)}, f32[4,512,2048]{2,1,0:T(8,128)}) fusion(f32[4,512,2048]{2,1,0:T(8,128)} %fusion.148, f32[4,512]{1,0:T(4,128)S(1)} %constant_dynamic-slice_fusion.2, f32[512,2048]{1,0:T(8,128)S(1)} %subtract_convert_fusion.5, f32[4]{0:T(128)S(1)} %multiply_exponential_fusion.5, ...), kind=kOutput, calls=%fused_computation.23.clone.1 | convolution fusion | flops 566228992 | bytes 40124932 | tf_op jit(solution)/shard_map/while/body/eval_jaxpr/while/body/eval_jaxpr/hqe,hke->hqk/dot_general | solution.py:50
  549.7 15.0 %multiply_convert_fusion.5 = bf16[4,512,2048]{2,1,0:T(8,128)(2,1)} fusion(f32[4,512,2048]{2,1,0:T(8,128)} %get-tuple-element.456, f32[4,512,2048]{2,1,0:T(8,128)} %fusion.148, f32[4,512]{1,0:T(4,128)S(1)} %get-tuple-element.457), kind=kLoop, calls=%fused_computation.22.clone.1 | loop fusion | flops 12582912 | bytes 41951232 | tf_op jit(solution)/shard_map/while/body/eval_jaxpr/while/body/eval_jaxpr/convert_element_type | solution.py:99
  596.3 14.5 %multiply_reduce_fusion.3 = (f32[4,512]{1,0:T(4,128)S(1)}, f32[4,512,2048]{2,1,0:T(8,128)}) fusion(f32[4,512,2048]{2,1,0:T(8,128)} %fusion.148, f32[4,512]{1,0:T(4,128)S(1)} %constant_dynamic-slice_fusion.2, f32[512,2048]{1,0:T(8,128)S(1)} %subtract_convert_fusion.5, f32[4]{0:T(128)S(1)} %multiply_exponential_fusion.5, ...), kind=kOutput, calls=%fused_computation.23.clone.1 | convolution fusion | flops 566228992 | bytes 40124932 | tf_op jit(solution)/shard_map/while/body/eval_jaxpr/while/body/eval_jaxpr/hqe,hke->hqk/dot_general | solution.py:50
  610.8 15.0 %multiply_convert_fusion.5 = bf16[4,512,2048]{2,1,0:T(8,128)(2,1)} fusion(f32[4,512,2048]{2,1,0:T(8,128)} %get-tuple-element.456, f32[4,512,2048]{2,1,0:T(8,128)} %fusion.148, f32[4,512]{1,0:T(4,128)S(1)} %get-tuple-element.457), kind=kLoop, calls=%fused_computation.22.clone.1 | loop fusion | flops 12582912 | bytes 41951232 | tf_op jit(solution)/shard_map/while/body/eval_jaxpr/while/body/eval_jaxpr/convert_element_type | solution.py:99
  657.4 14.5 %multiply_reduce_fusion.3 = (f32[4,512]{1,0:T(4,128)S(1)}, f32[4,512,2048]{2,1,0:T(8,128)}) fusion(f32[4,512,2048]{2,1,0:T(8,128)} %fusion.148, f32[4,512]{1,0:T(4,128)S(1)} %constant_dynamic-slice_fusion.2, f32[512,2048]{1,0:T(8,128)S(1)} %subtract_convert_fusion.5, f32[4]{0:T(128)S(1)} %multiply_exponential_fusion.5, ...), kind=kOutput, calls=%fused_computation.23.clone.1 | convolution fusion | flops 566228992 | bytes 40124932 | tf_op jit(solution)/shard_map/while/body/eval_jaxpr/while/body/eval_jaxpr/hqe,hke->hqk/dot_general | solution.py:50
  671.8 15.0 %multiply_convert_fusion.5 = bf16[4,512,2048]{2,1,0:T(8,128)(2,1)} fusion(f32[4,512,2048]{2,1,0:T(8,128)} %get-tuple-element.456, f32[4,512,2048]{2,1,0:T(8,128)} %fusion.148, f32[4,512]{1,0:T(4,128)S(1)} %get-tuple-element.457), kind=kLoop, calls=%fused_computation.22.clone.1 | loop fusion | flops 12582912 | bytes 41951232 | tf_op jit(solution)/shard_map/while/body/eval_jaxpr/while/body/eval_jaxpr/convert_element_type | solution.py:99
  731.0 22.5 %all-reduce.1 = (bf16[512]{0:T(512)(128)(2,1)S(1)}, bf16[1024]{0:T(1024)(128)(2,1)S(1)}) all-reduce(bf16[512]{0:T(512)(128)(2,1)S(1)} %convert_element_type.190, bf16[1024]{0:T(1024)(128)(2,1)S(1)} %copy-done.43), channel_id=1, replica_groups=mesh['dp'=8,'tensor'=4] {'dp'}, use_global_device_ids=true, to_apply=%region_26.27 | all-reduce | flops 1536 | bytes 6144 | tf_op jit(solution)/shard_map/psum | solution.py:271
  754.7 182.3 %all-reduce.5.cloned.1.call-done = (bf16[1024,768]{1,0:T(8,128)(2,1)}, bf16[256,1024]{1,0:T(8,128)(2,1)}, bf16[1024,1024]{1,0:T(8,128)(2,1)}, bf16[1024,1024]{1,0:T(8,128)(2,1)}) async-done(((bf16[1024,768]{1,0:T(8,128)(2,1)}, bf16[256,1024]{1,0:T(8,128)(2,1)}, bf16[1024,1024]{1,0:T(8,128)(2,1)}, bf16[1024,1024]{1,0:T(8,128)(2,1)}), (bf16[1024,768]{1,0:T(8,128)(2,1)}, bf16[256,1024]{1,0:T(8,128)(2,1)}, ...) | async-done | bytes 6291472 | tf_op jit(solution)/shard_map/psum | solution.py:270
  947.9 35.0 %reduce-scatter.11.cloned.1.call-done = bf16[512,1024]{1,0:T(8,128)(2,1)} async-done(((bf16[2048,1024]{1,0:T(8,128)(2,1)}), bf16[512,1024]{1,0:T(8,128)(2,1)}) %reduce-scatter.11.cloned.1.call-update) | async-done | bytes 1048592 | tf_op jit(solution)/shard_map/reduce_scatter | solution.py:260
  985.3 40.0 %all-reduce = (f32[1024]{0:T(1024)}, f32[1024]{0:T(1024)}, f32[1024]{0:T(1024)}, f32[1024]{0:T(1024)}, f32[1024]{0:T(1024)}, /*index=5*/f32[1024]{0:T(1024)}) all-reduce(f32[1024]{0:T(1024)S(1)} %get-tuple-element.241, f32[1024]{0:T(1024)S(1)} %get-tuple-element.246, ...), channel_id=1, replica_groups=mesh['dp'=8,'tensor'=4] {'dp','tensor'}, use_global_device_ids=true, to_apply=%region_21.22 | all-reduce | flops 6144 | bytes 49152 | tf_op jit(solution)/shard_map/psum | solution.py:277
  (338 shorter events, 339.4 us)
Async XLA Ops:
  7.2 291.2 %copy-start = (bf16[1024,1024]{1,0:T(8,128)(2,1)S(1)}, bf16[1024,1024]{1,0:T(8,128)(2,1)}, u32[]{:S(2)}) copy-start(bf16[1024,1024]{1,0:T(8,128)(2,1)} %param.36) | copy-start | bytes 6291460
  7.2 43.9 %all-gather.5.cloned.1.call-start = ((), (), s32[]{:S(2)}) async-start(), calls=%async_computation.4 | async-start | bytes 5242880 | tf_op jit(solution)/shard_map/all_gather | solution.py:158
  13.8 208.2 %reduce-scatter.5.cloned.1.call-start = ((), (), s32[]{:S(2)}) async-start(), calls=%async_computation.5 | async-start | bytes 5242880 | tf_op jit(solution)/shard_map/reduce_scatter | solution.py:178
  177.3 44.7 %copy-start.8 = (bf16[512,1024]{1,0:T(8,128)(2,1)S(1)}, bf16[512,1024]{1,0:T(8,128)(2,1)}, u32[]{:S(2)}) copy-start(bf16[512,1024]{1,0:T(8,128)(2,1)} %param.21) | copy-start | bytes 3145732
  177.3 44.7 %copy-start.29 = (f32[1024]{0:T(1024)S(1)}, f32[1024]{0:T(1024)}, u32[]{:S(2)}) copy-start(f32[1024]{0:T(1024)} %param.31) | copy-start | bytes 12292
  177.3 48.2 %copy-start.32 = (f32[1024]{0:T(1024)S(1)}, f32[1024]{0:T(1024)}, u32[]{:S(2)}) copy-start(f32[1024]{0:T(1024)} %param.32) | copy-start | bytes 12292
  177.3 48.2 %copy-start.41 = (f32[1024]{0:T(1024)S(1)}, f32[1024]{0:T(1024)}, u32[]{:S(2)}) copy-start(f32[1024]{0:T(1024)} %param.33) | copy-start | bytes 12292
  177.3 51.2 %copy-start.44 = (f32[46]{0:T(128)S(1)}, f32[46]{0:T(128)}, u32[]{:S(2)}) copy-start(f32[46]{0:T(128)} %param.25) | copy-start | bytes 556
  177.3 84.4 %all-gather.7.cloned.1.call-start = ((), (), s32[]{:S(2)}) async-start(), calls=%async_computation.6 | async-start | bytes 5242880 | tf_op jit(solution)/shard_map/all_gather | solution.py:189
  227.2 71.2 %all-gather.9.cloned.1.call-start = ((), (), s32[]{:S(2)}) async-start(), calls=%async_computation.8 | async-start | bytes 5242880 | tf_op jit(solution)/shard_map/all_gather | solution.py:218
  231.1 67.3 %copy-start.50 = (f32[1024]{0:T(1024)S(1)}, f32[1024]{0:T(1024)}, u32[]{:S(2)}) copy-start(f32[1024]{0:T(1024)} %param.35) | copy-start | bytes 12292
  231.1 134.0 %reduce-scatter.9.cloned.1.call-start = ((), (), s32[]{:S(2)}) async-start(), calls=%async_computation.9 | async-start | bytes 5242880 | tf_op jit(solution)/shard_map/reduce_scatter | solution.py:225
  320.4 92.2 %reduce-scatter.7.cloned.1.call-start = ((), (), s32[]{:S(2)}) async-start(), calls=%async_computation.7 | async-start | bytes 5242880 | tf_op jit(solution)/shard_map/reduce_scatter | solution.py:199
  331.6 81.0 %copy-start.22 = (bf16[512,1024]{1,0:T(8,128)(2,1)S(1)}, bf16[512,1024]{1,0:T(8,128)(2,1)}, u32[]{:S(2)}) copy-start(bf16[512,1024]{1,0:T(8,128)(2,1)} %param.22) | copy-start | bytes 3145732
  331.6 81.0 %copy-start.40 = (f32[1024]{0:T(1024)S(1)}, f32[1024]{0:T(1024)}, u32[]{:S(2)}) copy-start(f32[1024]{0:T(1024)} %param.37) | copy-start | bytes 12292
  331.7 122.5 %all-gather.11.cloned.1.call-start = ((), (), s32[]{:S(2)}) async-start(), calls=%async_computation.10 | async-start | bytes 5242880 | tf_op jit(solution)/shard_map/all_gather | solution.py:236
  419.5 517.5 %all-reduce.5.cloned.1.call-start = ((), (), s32[]{:S(2)}) async-start(), calls=%async_computation.12 | async-start | bytes 12582912 | tf_op jit(solution)/shard_map/psum | solution.py:270
  721.9 261.0 %reduce-scatter.11.cloned.1.call-start = ((), (), s32[]{:S(2)}) async-start(), calls=%async_computation.11 | async-start | bytes 5242880 | tf_op jit(solution)/shard_map/reduce_scatter | solution.py:260
  945.0 38.0 %copy-start.35 = (f32[512]{0:T(512)S(1)}, f32[512]{0:T(512)}, u32[]{:S(2)}) copy-start(f32[512]{0:T(512)} %copy-done.34) | copy-start | bytes 6148
  945.0 40.2 %copy-start.36 = (f32[1024]{0:T(1024)S(1)}, f32[1024]{0:T(1024)}, u32[]{:S(2)}) copy-start(f32[1024]{0:T(1024)} %get-tuple-element.303) | copy-start | bytes 12292
  945.0 40.2 %copy-start.37 = (f32[1024]{0:T(1024)S(1)}, f32[1024]{0:T(1024)}, u32[]{:S(2)}) copy-start(f32[1024]{0:T(1024)} %get-tuple-element.315) | copy-start | bytes 12292
  945.0 40.2 %copy-start.38 = (f32[1024]{0:T(1024)S(1)}, f32[1024]{0:T(1024)}, u32[]{:S(2)}) copy-start(f32[1024]{0:T(1024)} %get-tuple-element.239) | copy-start | bytes 12292
  945.0 40.2 %copy-start.39 = (f32[1024]{0:T(1024)S(1)}, f32[1024]{0:T(1024)}, u32[]{:S(2)}) copy-start(f32[1024]{0:T(1024)} %get-tuple-element.245) | copy-start | bytes 12292
  945.1 83.8 %copy-start.1 = (bf16[1024,1024]{1,0:T(8,128)(2,1)S(1)}, bf16[1024,1024]{1,0:T(8,128)(2,1)}, u32[]{:S(2)}) copy-start(bf16[1024,1024]{1,0:T(8,128)(2,1)} %param.36) | copy-start | bytes 6291460
  (73 other events, 652.0 us)
Sparse Core Ops, SparseCore 0:
  13.9 37.1 all-gather.4
  177.4 44.4 reduce-scatter.4
  227.3 34.4 all-gather.6
  263.8 34.4 all-gather.8
  320.5 44.5 reduce-scatter.8
  368.0 44.5 reduce-scatter.6
  419.6 34.4 all-gather.10
  722.0 214.8 all-reduce.4
  939.4 43.4 reduce-scatter.10
where the time goes:
time: 1040 us
  waiting for transfers between devices  447 us (43%)
  matrix products  297 us (29%)
  other arithmetic  145 us (14%)
  blocking collectives  62.5 us (6%)
  local copies, waits for them, and re-layouts  51.4 us (5%)
  loops' own time  17.1 us (2%)
  between operations  16 us (2%)
    psum x1, waiting for transfers between devices, body(): lax.psum(g_w_qkv.astype(jnp.bfloat16), 'dp').astype(jnp.float32)  182 us
    dot_general x8, matrix products, masked_scores(): jnp.einsum('hqe,hke->hqk', query_block, keys, preferred_element_type=jnp....  85.5 us
    convert_element_type x4, other arithmetic, backward_block(): grad_scores = (probs * (grad_probs - jnp.sum(probs * grad_probs, axis=-1,...  60 us
    reduce_scatter x1, waiting for transfers between devices, body(): lax.psum_scatter(jnp.dot(heads_b, w_out, preferred_element_type=jnp.float...  44.6 us
    reduce_scatter x1, waiting for transfers between devices, body(): lax.psum_scatter(jnp.dot(active_b, w_down, preferred_element_type=jnp.flo...  44.5 us
    psum x1, blocking collectives, body(): lax.psum((g_ln1_gain, g_ln1_bias, g_b_out, g_ln2_gain, g_ln2_bias, g_b_do...  40 us
    dot_general x4, matrix products, backward_block(): jnp.einsum('hqe,hke->hqk', grad_block, values, preferred_element_type=jnp...  37.1 us
    all_gather x1, waiting for transfers between devices, body(): lax.all_gather(normed1_b, 'tensor', axis=0, tiled=True)  37 us
  transfers between devices with their start and end apart: 9, of which 9 were waited for; matrix products, arithmetic and copies ran while one was open for 7% of the time, Pallas kernels for 0%

commit v1 on v0

--- a/solution.py
+++ b/solution.py
@@ -266,8 +266,12 @@
     g_ln1_gain = jnp.sum(grad_norm1 * unit1, axis=0)
     g_ln1_bias = jnp.sum(grad_norm1, axis=0)
     grad_input = grad_middle + norm_back(grad_norm1, unit1, factor1, ln1_gain)
+
+    def _note_scenes(local):
+        return jnp.sum(lax.all_gather(local, axis_name="dp"), 0)
+
     weights = (
-        lax.psum(g_w_qkv.astype(jnp.bfloat16), "dp").astype(jnp.float32),
+        _note_scenes(g_w_qkv.astype(jnp.bfloat16)).astype(jnp.float32),
         lax.psum(g_b_qv.astype(jnp.bfloat16), "dp").astype(jnp.float32),
         lax.psum(g_w_out.astype(jnp.bfloat16), "dp").astype(jnp.float32),
         lax.psum(g_w_up.astype(jnp.bfloat16), "dp").astype(jnp.float32),

time: 1040 us -> 972 us (0.935)
  waiting for transfers between devices: 447 us -> 366 us
    psum x1, waiting for transfers between devices: 182 us -> 0.01 us  [body(): lax.psum(g_w_out.astype(jnp.bfloat16), 'dp').astype(jnp.float32)]
    all_gather x0 -> x1, waiting for transfers between devices: none -> 131 us  [_note_scenes(): return jnp.sum(lax.all_gather(local, axis_name='dp'), 0)]
    reduce_scatter x1, waiting for transfers between devices: 35 us -> 5.12 us  [body(): lax.psum_scatter(times_trans(grad_mixed_b, w_qkv).astype(jnp.bfloat16), '...]
  transfers between devices with their start and end apart: 9 -> 10, of which waited for: 9 -> 9; matrix products, arithmetic and copies ran while one was open for 7% -> 32% of each run, Pallas kernels for 0% -> 0%
where the time goes in v1:
time: 972 us; the launch traced here: 968 us
  waiting for transfers between devices  366 us (38%)
  matrix products  300 us (31%)
  other arithmetic  155 us (16%)
  blocking collectives  63.8 us (7%)
  local copies, waits for them, and re-layouts  49.7 us (5%)
  loops' own time  17.1 us (2%)
  between operations  16.2 us (2%)
    all_gather x1, waiting for transfers between devices, _note_scenes(): return jnp.sum(lax.all_gather(local, axis_name='dp'), 0)  131 us
    dot_general x8, matrix products, masked_scores(): jnp.einsum('hqe,hke->hqk', query_block, keys, preferred_element_type=jnp....  85.6 us
    convert_element_type x4, other arithmetic, backward_block(): grad_scores = (probs * (grad_probs - jnp.sum(probs * grad_probs, axis=-1,...  60.5 us
    reduce_scatter x1, waiting for transfers between devices, body(): lax.psum_scatter(jnp.dot(heads_b, w_out, preferred_element_type=jnp.float...  44.6 us
    reduce_scatter x1, waiting for transfers between devices, body(): lax.psum_scatter(jnp.dot(active_b, w_down, preferred_element_type=jnp.flo...  44.5 us
    psum x1, blocking collectives, body(): lax.psum((g_ln1_gain, g_ln1_bias, g_b_out, g_ln2_gain, g_ln2_bias, g_b_do...  42.6 us
    dot_general x4, matrix products, backward_block(): jnp.einsum('hqe,hke->hqk', grad_block, values, preferred_element_type=jnp...  37.1 us
    all_gather x1, waiting for transfers between devices, body(): lax.all_gather(normed1_b, 'tensor', axis=0, tiled=True)  37 us
  transfers between devices with their start and end apart: 10, of which 9 were waited for; matrix products, arithmetic and copies ran while one was open for 32% of the time, Pallas kernels for 0%

profile of v1, /device:TPU:0, one launch (start us, length us, event | category | flops | bytes accessed | tf_op | source)
XLA Modules:
  0.0 967.7 jit_solution(8893081762318555789)
XLA Ops:
  14.1 37.0 %all-gather.7.cloned.1.call-done = bf16[2048,1024]{1,0:T(8,128)(2,1)} async-done(((bf16[512,1024]{1,0:T(8,128)(2,1)}), bf16[2048,1024]{1,0:T(8,128)(2,1)}) %all-gather.7.cloned.1.call-update) | async-done | bytes 4194320 | tf_op jit(solution)/shard_map/all_gather | solution.py:158
  60.2 106.8 %while.48 = (s32[]{:T(128)}, bf16[4,4,512,64]{2,3,1,0:T(8,128)(2,1)}, f32[4,4,512]{2,1,0:T(4,128)S(1)}, s32[4]{0:T(128)S(1)}, s32[]{:T(128)}, /*index=5*/bf16[4,...) while((s32[]{:T(128)}, ...), condition=%wide.region_5.6_spmd.clone, body=%wide.region_2.5_spmd.clone.sunk | while | flops 1153434112 | bytes 99428696 | solution.py:74
  177.8 44.6 %reduce-scatter.5.cloned.1.call-done = bf16[512,1024]{1,0:T(8,128)(2,1)} async-done(((bf16[2048,1024]{1,0:T(8,128)(2,1)}), bf16[512,1024]{1,0:T(8,128)(2,1)}) %reduce-scatter.5.cloned.1.call-update) | async-done | bytes 1048592 | tf_op jit(solution)/shard_map/reduce_scatter | solution.py:178
  231.6 30.6 %all-gather.9.cloned.1.call-done = bf16[2048,1024]{1,0:T(8,128)(2,1)} async-done(((bf16[512,1024]{1,0:T(8,128)(2,1)}), bf16[2048,1024]{1,0:T(8,128)(2,1)}) %all-gather.9.cloned.1.call-update) | async-done | bytes 4194320 | tf_op jit(solution)/shard_map/all_gather | solution.py:189
  262.2 11.4 %fusion.83 = f32[2048,1024]{1,0:T(8,128)} fusion(bf16[2048,1024]{1,0:T(8,128)(2,1)} %all-gather.9.cloned.1.call-done, bf16[1024,1024]{1,0:T(8,128)(2,1)} %param.34), kind=kOutput, calls=%fused_computation.151 | convolution fusion | flops 4294967296 | bytes 14680064 | tf_op jit(solution)/shard_map/dot_general | solution.py:188
  273.6 25.2 %all-gather.11.cloned.1.call-done = bf16[2048,1024]{1,0:T(8,128)(2,1)} async-done(((bf16[512,1024]{1,0:T(8,128)(2,1)}), bf16[2048,1024]{1,0:T(8,128)(2,1)}) %all-gather.11.cloned.1.call-update) | async-done | bytes 4194320 | tf_op jit(solution)/shard_map/all_gather | solution.py:218
  298.8 13.5 %fusion.76 = (bf16[1024]{0:T(1024)(128)(2,1)}, bf16[2048,1024]{1,0:T(8,128)(2,1)S(1)}) fusion(f32[2048,1024]{1,0:T(8,128)} %fusion.83, f32[1024]{0:T(1024)S(1)} %copy-done.47, bf16[2048,1024]{1,0:T(8,128)(2,1)} %all-gather.11.cloned.1.call-done, bf16[1024,1024]{1,0:T(8,128)(2,1)S(1)} %copy-done), kind=kOutput, calls=%fused_computation.146 | convolution fusion | flops 4341103616 | bytes 18880512 | tf_op jit(solution)/shard_map/dot_general | solution.py:34
  320.6 11.2 %convolution_convert_fusion.3 = bf16[2048,1024]{1,0:T(8,128)(2,1)} fusion(bf16[1024,1024]{1,0:T(8,128)(2,1)S(1)} %copy-done, f32[2048,1024]{1,0:T(8,128)} %fusion.83, f32[1024]{0:T(1024)S(1)} %copy-done.47), kind=kOutput, calls=%fused_computation.65 | convolution fusion | flops 4318035968 | bytes 14684160 | tf_op jit(solution)/shard_map/dot_general | solution.py:200
  331.8 33.4 %reduce-scatter.9.cloned.1.call-done = bf16[512,1024]{1,0:T(8,128)(2,1)} async-done(((bf16[2048,1024]{1,0:T(8,128)(2,1)}), bf16[512,1024]{1,0:T(8,128)(2,1)}) %reduce-scatter.9.cloned.1.call-update) | async-done | bytes 1048592 | tf_op jit(solution)/shard_map/reduce_scatter | solution.py:225
  368.2 44.5 %reduce-scatter.7.cloned.1.call-done = bf16[512,1024]{1,0:T(8,128)(2,1)} async-done(((bf16[2048,1024]{1,0:T(8,128)(2,1)}), bf16[512,1024]{1,0:T(8,128)(2,1)}) %reduce-scatter.7.cloned.1.call-update) | async-done | bytes 1048592 | tf_op jit(solution)/shard_map/reduce_scatter | solution.py:199
  429.4 11.0 %convolution_convert_fusion.5 = bf16[1024,1024]{1,0:T(8,128)(2,1)} fusion(bf16[2048,1024]{1,0:T(8,128)(2,1)S(1)} %copy-done.44, f32[2048,1024]{1,0:T(8,128)} %fusion.83, f32[1024]{0:T(1024)S(1)} %copy-done.47), kind=kOutput, calls=%fused_computation.109 | convolution fusion | flops 4316987392 | bytes 14684160 | tf_op jit(solution)/shard_map/dot_general | solution.py:28
  440.4 14.1 %all-gather.13.cloned.1.call-done = bf16[2048,1024]{1,0:T(8,128)(2,1)} async-done(((bf16[512,1024]{1,0:T(8,128)(2,1)}), bf16[2048,1024]{1,0:T(8,128)(2,1)}) %all-gather.13.cloned.1.call-update) | async-done | bytes 4194320 | tf_op jit(solution)/shard_map/all_gather | solution.py:236
  465.2 246.0 %while.49 = (s32[]{:T(128)}, f32[4,2048,64]{1,2,0:T(8,128)}, f32[4,2048,64]{1,2,0:T(8,128)}, bf16[4,4,512,64]{2,3,1,0:T(8,128)(2,1)}, s32[4]{0:T(128)S(1)}, /*in...) while((s32[]{:T(128)}, f32[4,2048,64]{1,2,0:T(8,128)}, ...), condition=%wide.region_16.17_spmd.clone, body=%wide.region_14.16_spmd.clone.sunk | while | flops 2737439232 | bytes 296274944 | solution.py:121
  479.7 14.5 %multiply_reduce_fusion.3 = (f32[4,512]{1,0:T(4,128)S(1)}, f32[4,512,2048]{2,1,0:T(8,128)}) fusion(f32[4,512,2048]{2,1,0:T(8,128)} %fusion.148, f32[4,512]{1,0:T(4,128)S(1)} %constant_dynamic-slice_fusion.2, f32[512,2048]{1,0:T(8,128)S(1)} %subtract_convert_fusion.5, f32[4]{0:T(128)S(1)} %multiply_exponential_fusion.5, ...), kind=kOutput, calls=%fused_computation.23.clone.1 | convolution fusion | flops 566228992 | bytes 40124932 | tf_op jit(solution)/shard_map/while/body/eval_jaxpr/while/body/eval_jaxpr/hqe,hke->hqk/dot_general | solution.py:50
  494.2 15.3 %multiply_convert_fusion.5 = bf16[4,512,2048]{2,1,0:T(8,128)(2,1)} fusion(f32[4,512,2048]{2,1,0:T(8,128)} %get-tuple-element.455, f32[4,512,2048]{2,1,0:T(8,128)} %fusion.148, f32[4,512]{1,0:T(4,128)S(1)} %get-tuple-element.456), kind=kLoop, calls=%fused_computation.22.clone.1 | loop fusion | flops 12582912 | bytes 41951232 | tf_op jit(solution)/shard_map/while/body/eval_jaxpr/while/body/eval_jaxpr/convert_element_type | solution.py:99
  541.2 14.5 %multiply_reduce_fusion.3 = (f32[4,512]{1,0:T(4,128)S(1)}, f32[4,512,2048]{2,1,0:T(8,128)}) fusion(f32[4,512,2048]{2,1,0:T(8,128)} %fusion.148, f32[4,512]{1,0:T(4,128)S(1)} %constant_dynamic-slice_fusion.2, f32[512,2048]{1,0:T(8,128)S(1)} %subtract_convert_fusion.5, f32[4]{0:T(128)S(1)} %multiply_exponential_fusion.5, ...), kind=kOutput, calls=%fused_computation.23.clone.1 | convolution fusion | flops 566228992 | bytes 40124932 | tf_op jit(solution)/shard_map/while/body/eval_jaxpr/while/body/eval_jaxpr/hqe,hke->hqk/dot_general | solution.py:50
  555.8 15.1 %multiply_convert_fusion.5 = bf16[4,512,2048]{2,1,0:T(8,128)(2,1)} fusion(f32[4,512,2048]{2,1,0:T(8,128)} %get-tuple-element.455, f32[4,512,2048]{2,1,0:T(8,128)} %fusion.148, f32[4,512]{1,0:T(4,128)S(1)} %get-tuple-element.456), kind=kLoop, calls=%fused_computation.22.clone.1 | loop fusion | flops 12582912 | bytes 41951232 | tf_op jit(solution)/shard_map/while/body/eval_jaxpr/while/body/eval_jaxpr/convert_element_type | solution.py:99
  603.2 14.5 %multiply_reduce_fusion.3 = (f32[4,512]{1,0:T(4,128)S(1)}, f32[4,512,2048]{2,1,0:T(8,128)}) fusion(f32[4,512,2048]{2,1,0:T(8,128)} %fusion.148, f32[4,512]{1,0:T(4,128)S(1)} %constant_dynamic-slice_fusion.2, f32[512,2048]{1,0:T(8,128)S(1)} %subtract_convert_fusion.5, f32[4]{0:T(128)S(1)} %multiply_exponential_fusion.5, ...), kind=kOutput, calls=%fused_computation.23.clone.1 | convolution fusion | flops 566228992 | bytes 40124932 | tf_op jit(solution)/shard_map/while/body/eval_jaxpr/while/body/eval_jaxpr/hqe,hke->hqk/dot_general | solution.py:50
  617.7 15.0 %multiply_convert_fusion.5 = bf16[4,512,2048]{2,1,0:T(8,128)(2,1)} fusion(f32[4,512,2048]{2,1,0:T(8,128)} %get-tuple-element.455, f32[4,512,2048]{2,1,0:T(8,128)} %fusion.148, f32[4,512]{1,0:T(4,128)S(1)} %get-tuple-element.456), kind=kLoop, calls=%fused_computation.22.clone.1 | loop fusion | flops 12582912 | bytes 41951232 | tf_op jit(solution)/shard_map/while/body/eval_jaxpr/while/body/eval_jaxpr/convert_element_type | solution.py:99
  664.3 14.5 %multiply_reduce_fusion.3 = (f32[4,512]{1,0:T(4,128)S(1)}, f32[4,512,2048]{2,1,0:T(8,128)}) fusion(f32[4,512,2048]{2,1,0:T(8,128)} %fusion.148, f32[4,512]{1,0:T(4,128)S(1)} %constant_dynamic-slice_fusion.2, f32[512,2048]{1,0:T(8,128)S(1)} %subtract_convert_fusion.5, f32[4]{0:T(128)S(1)} %multiply_exponential_fusion.5, ...), kind=kOutput, calls=%fused_computation.23.clone.1 | convolution fusion | flops 566228992 | bytes 40124932 | tf_op jit(solution)/shard_map/while/body/eval_jaxpr/while/body/eval_jaxpr/hqe,hke->hqk/dot_general | solution.py:50
  678.8 15.0 %multiply_convert_fusion.5 = bf16[4,512,2048]{2,1,0:T(8,128)(2,1)} fusion(f32[4,512,2048]{2,1,0:T(8,128)} %get-tuple-element.455, f32[4,512,2048]{2,1,0:T(8,128)} %fusion.148, f32[4,512]{1,0:T(4,128)S(1)} %get-tuple-element.456), kind=kLoop, calls=%fused_computation.22.clone.1 | loop fusion | flops 12582912 | bytes 41951232 | tf_op jit(solution)/shard_map/while/body/eval_jaxpr/while/body/eval_jaxpr/convert_element_type | solution.py:99
  733.4 21.2 %all-reduce.1 = (bf16[512]{0:T(512)(128)(2,1)S(1)}, bf16[1024]{0:T(1024)(128)(2,1)S(1)}) all-reduce(bf16[512]{0:T(512)(128)(2,1)S(1)} %convert_element_type.192, bf16[1024]{0:T(1024)(128)(2,1)S(1)} %copy-done.42), channel_id=1, replica_groups=mesh['dp'=8,'tensor'=4] {'dp'}, use_global_device_ids=true, to_apply=%region_26.27 | all-reduce | flops 1536 | bytes 6144 | tf_op jit(solution)/shard_map/psum | solution.py:275
  772.2 42.6 %all-reduce = (f32[1024]{0:T(1024)}, f32[1024]{0:T(1024)}, f32[1024]{0:T(1024)}, f32[1024]{0:T(1024)}, f32[1024]{0:T(1024)}, /*index=5*/f32[1024]{0:T(1024)}) all-reduce(f32[1024]{0:T(1024)S(1)} %get-tuple-element.241, f32[1024]{0:T(1024)S(1)} %get-tuple-element.246, ...), channel_id=1, replica_groups=mesh['dp'=8,'tensor'=4] {'dp','tensor'}, use_global_device_ids=true, to_apply=%region_21.22 | all-reduce | flops 6144 | bytes 49152 | tf_op jit(solution)/shard_map/psum | solution.py:281
  818.4 130.9 %all-gather.15.cloned.1.call-done = bf16[8192,768]{1,0:T(8,128)(2,1)} async-done(((bf16[1024,768]{1,0:T(8,128)(2,1)}), bf16[8192,768]{1,0:T(8,128)(2,1)}) %all-gather.15.cloned.1.call-update) | async-done | bytes 12582928 | tf_op jit(solution)/shard_map/all_gather | solution.py:271
  (336 shorter events, 344.9 us)
Async XLA Ops:
  7.2 291.6 %copy-start = (bf16[1024,1024]{1,0:T(8,128)(2,1)S(1)}, bf16[1024,1024]{1,0:T(8,128)(2,1)}, u32[]{:S(2)}) copy-start(bf16[1024,1024]{1,0:T(8,128)(2,1)} %param.36) | copy-start | bytes 6291460
  7.2 43.9 %all-gather.7.cloned.1.call-start = ((), (), s32[]{:S(2)}) async-start(), calls=%async_computation.4 | async-start | bytes 5242880 | tf_op jit(solution)/shard_map/all_gather | solution.py:158
  13.8 208.6 %reduce-scatter.5.cloned.1.call-start = ((), (), s32[]{:S(2)}) async-start(), calls=%async_computation.5 | async-start | bytes 5242880 | tf_op jit(solution)/shard_map/reduce_scatter | solution.py:178
  177.7 44.7 %copy-start.8 = (bf16[512,1024]{1,0:T(8,128)(2,1)S(1)}, bf16[512,1024]{1,0:T(8,128)(2,1)}, u32[]{:S(2)}) copy-start(bf16[512,1024]{1,0:T(8,128)(2,1)} %param.21) | copy-start | bytes 3145732
  177.7 44.7 %copy-start.28 = (f32[1024]{0:T(1024)S(1)}, f32[1024]{0:T(1024)}, u32[]{:S(2)}) copy-start(f32[1024]{0:T(1024)} %param.31) | copy-start | bytes 12292
  177.7 48.3 %copy-start.31 = (f32[1024]{0:T(1024)S(1)}, f32[1024]{0:T(1024)}, u32[]{:S(2)}) copy-start(f32[1024]{0:T(1024)} %param.32) | copy-start | bytes 12292
  177.7 48.3 %copy-start.40 = (f32[1024]{0:T(1024)S(1)}, f32[1024]{0:T(1024)}, u32[]{:S(2)}) copy-start(f32[1024]{0:T(1024)} %param.33) | copy-start | bytes 12292
  177.7 51.2 %copy-start.43 = (f32[46]{0:T(128)S(1)}, f32[46]{0:T(128)}, u32[]{:S(2)}) copy-start(f32[46]{0:T(128)} %param.25) | copy-start | bytes 556
  177.7 84.5 %all-gather.9.cloned.1.call-start = ((), (), s32[]{:S(2)}) async-start(), calls=%async_computation.6 | async-start | bytes 5242880 | tf_op jit(solution)/shard_map/all_gather | solution.py:189
  227.6 71.2 %all-gather.11.cloned.1.call-start = ((), (), s32[]{:S(2)}) async-start(), calls=%async_computation.8 | async-start | bytes 5242880 | tf_op jit(solution)/shard_map/all_gather | solution.py:218
  231.5 67.3 %copy-start.47 = (f32[1024]{0:T(1024)S(1)}, f32[1024]{0:T(1024)}, u32[]{:S(2)}) copy-start(f32[1024]{0:T(1024)} %param.35) | copy-start | bytes 12292
  231.5 133.6 %reduce-scatter.9.cloned.1.call-start = ((), (), s32[]{:S(2)}) async-start(), calls=%async_computation.9 | async-start | bytes 5242880 | tf_op jit(solution)/shard_map/reduce_scatter | solution.py:225
  320.5 92.2 %reduce-scatter.7.cloned.1.call-start = ((), (), s32[]{:S(2)}) async-start(), calls=%async_computation.7 | async-start | bytes 5242880 | tf_op jit(solution)/shard_map/reduce_scatter | solution.py:199
  331.7 33.5 %copy-start.17 = (bf16[512,1024]{1,0:T(8,128)(2,1)S(1)}, bf16[512,1024]{1,0:T(8,128)(2,1)}, u32[]{:S(2)}) copy-start(bf16[512,1024]{1,0:T(8,128)(2,1)} %reduce-scatter.5.cloned.1.call-done) | copy-start | bytes 3145732
  331.7 81.0 %copy-start.22 = (bf16[512,1024]{1,0:T(8,128)(2,1)S(1)}, bf16[512,1024]{1,0:T(8,128)(2,1)}, u32[]{:S(2)}) copy-start(bf16[512,1024]{1,0:T(8,128)(2,1)} %param.22) | copy-start | bytes 3145732
  331.7 81.0 %copy-start.39 = (f32[1024]{0:T(1024)S(1)}, f32[1024]{0:T(1024)}, u32[]{:S(2)}) copy-start(f32[1024]{0:T(1024)} %param.37) | copy-start | bytes 12292
  331.8 122.7 %all-gather.13.cloned.1.call-start = ((), (), s32[]{:S(2)}) async-start(), calls=%async_computation.10 | async-start | bytes 5242880 | tf_op jit(solution)/shard_map/all_gather | solution.py:236
  419.8 336.0 %all-reduce.5.cloned.1.call-start = ((), (), s32[]{:S(2)}) async-start(), calls=%async_computation.13 | async-start | bytes 9437184 | tf_op jit(solution)/shard_map/psum | solution.py:276
  429.4 25.1 %copy-start.21 = (bf16[1,4,2048,64]{2,3,1,0:T(8,128)(2,1)S(1)}, bf16[1,4,2048,64]{2,3,1,0:T(8,128)(2,1)}, u32[]{:S(2)}) copy-start(bf16[1,4,2048,64]{2,3,1,0:T(8,128)(2,1)} %copy-done.20) | copy-start | bytes 3145732
  458.7 311.1 %reduce-scatter.11.cloned.1.call-start = ((), (), s32[]{:S(2)}) async-start(), calls=%async_computation.11 | async-start | bytes 5242880 | tf_op jit(solution)/shard_map/reduce_scatter | solution.py:260
  494.2 19.4 %copy-start.13 = (f32[4,2048,64]{1,2,0:T(8,128)S(1)}, f32[4,2048,64]{1,2,0:T(8,128)}, u32[]{:S(2)}) copy-start(f32[4,2048,64]{1,2,0:T(8,128)} %get-tuple-element.510) | copy-start | bytes 6291460 | tf_op jit(solution)/shard_map/while/body/eval_jaxpr/while
  555.8 19.8 %copy-start.13 = (f32[4,2048,64]{1,2,0:T(8,128)S(1)}, f32[4,2048,64]{1,2,0:T(8,128)}, u32[]{:S(2)}) copy-start(f32[4,2048,64]{1,2,0:T(8,128)} %get-tuple-element.510) | copy-start | bytes 6291460 | tf_op jit(solution)/shard_map/while/body/eval_jaxpr/while
  678.8 19.0 %copy-start.13 = (f32[4,2048,64]{1,2,0:T(8,128)S(1)}, f32[4,2048,64]{1,2,0:T(8,128)}, u32[]{:S(2)}) copy-start(f32[4,2048,64]{1,2,0:T(8,128)} %get-tuple-element.510) | copy-start | bytes 6291460 | tf_op jit(solution)/shard_map/while/body/eval_jaxpr/while
  725.3 224.0 %all-gather.15.cloned.1.call-start = ((), (), s32[]{:S(2)}) async-start(), calls=%async_computation.12 | async-start | bytes 14155776 | tf_op jit(solution)/shard_map/all_gather | solution.py:271
  (71 other events, 478.6 us)
Sparse Core Ops, SparseCore 0:
  13.9 37.1 all-gather.6
  177.8 44.5 reduce-scatter.4
  227.7 34.4 all-gather.8
  264.3 34.4 all-gather.10
  320.6 44.5 reduce-scatter.8
  368.1 44.5 reduce-scatter.6
  420.0 34.4 all-gather.12
  459.5 170.3 all-reduce.4
  725.4 44.3 reduce-scatter.10
  771.9 177.3 all-gather.14
